TPU v7x, 512 devices: a whole 4x4x16 slice. The times are simulated.
512 devices in a mesh: space: 32 (over z, x_lo), field: 16 (over x_hi, y, core).
Axes of the slice: x: 4 (x_hi: 2, x_lo: 2; x = x_hi * 2 + x_lo), y: 4, z: 16, core: 2. Of those that a mesh axis runs over, the one named last changes fastest.
Arguments:
- composition_vector: float32 [16, 32, 128, 16, 128], P('field', None, 'space'), may hold values from -6 to 6
- filtered_motion: float32 [3, 128, 16, 128], P(None, 'space', 'field'), may hold values from -1.8 to 1.8
- spreading_strength: float32 [128, 16, 128], P('space', 'field'), may hold values from 0.02 to 0.12
- blend_relax_multiplier: float32 [128, 16, 128], P('space', 'field'), may hold values from 0.2 to 0.9
- thermal_level: float32 [128, 16, 128], P('space', 'field'), may hold values from 0.5 to 2
- brownian_jumps: float32 [2, 16, 3], P(None, 'field'), may hold values from -2.5 to 2.5
- left_bilinear_weights: bfloat16 [206, 32], replicated, may hold values from -1 to 1
- right_bilinear_weights: bfloat16 [206, 32], replicated, may hold values from -1 to 1
- species_yield_weights: bfloat16 [32, 206], replicated, may hold values from -0.4375 to 0.4375
- arrhenius_prefactor: float32 [206], replicated, may hold values from 0.3 to 3
- ignition_energy_ratio: float32 [206], replicated, may hold values from 0.2 to 2
Outputs:
- result: float32 [16, 32, 128, 16, 128], P('field', None, 'space')
All inputs are finite; a program needn't handle non-finite values.
Results may differ from a plain program's by a relative error of at most 0.00068.
Values sent between devices are 32-bit elements; how exact they have to be, the bound alone decides.
No kernel may reach another device: no remote copies, remote signals or barrier semaphores. Data moves between devices by JAX's collectives and lax.ppermute only.
A program may use at most 64 MiB of HBM per device.

v0:
```python
import jax
import jax.numpy as jnp
from jax import lax
from jax.sharding import PartitionSpec as P

STEPS = 2
SUB = 5


chem_step = 0.2


def turned_gather(arrays, axis, dims):
    turned = [jnp.moveaxis(a, dim, 0) for a, dim in zip(arrays, dims)]
    widths = [t[0].size for t in turned]
    both = jnp.concatenate([t.reshape(-1, w) for t, w in zip(turned, widths)], axis=1)
    result = lax.all_gather(both, axis, axis=0, tiled=True)
    tiles = jnp.split(result, [sum(widths[:k]) for k in range(1, len(widths))], axis=1)
    return tuple(
        (
            jnp.moveaxis(b.reshape(-1, *t.shape[1:]), 0, dim)
            for b, t, dim in zip(tiles, turned, dims)
        )
    )


def split_up(value, dim, count):
    dims = value.shape
    tiles = value.reshape(*dims[:dim], count, dims[dim] // count, *dims[dim + 1 :])
    return jnp.moveaxis(tiles, dim, 0)


def sent_and_summed(value, axis, dim):
    tiles = split_up(value, dim, lax.axis_size(axis))
    arrived = lax.all_to_all(tiles, axis, split_axis=0, concat_axis=0, tiled=True)
    return arrived.sum(axis=0)


def laid_out(tiles, dim):
    dims = list(tiles.shape[1:])
    dims[dim] *= tiles.shape[0]
    return jnp.moveaxis(tiles, 0, dim).reshape(dims)


def from_everyone(value, axis):
    count = lax.axis_size(axis)
    return lax.all_to_all(
        jnp.broadcast_to(value[None], (count, *value.shape)), axis, 0, 0, tiled=True
    )


def collect(value, axis, dim):
    return laid_out(from_everyone(value, axis), dim)


def extended(value, sides, width):
    for axis, dim in sides:
        count, length = (lax.axis_size(axis), value.shape[dim])
        up = [(i, (i + 1) % count) for i in range(count)]
        down = [(j, i) for i, j in up]
        last = lax.slice_in_dim(value, length - width, length, axis=dim)
        leading = lax.slice_in_dim(value, 0, width, axis=dim)
        before = lax.ppermute(last, axis, up)
        after = lax.ppermute(leading, axis, down)
        value = jnp.concatenate([before, value, after], axis=dim)
    return value


def transport(padded, current, mean, filtered_motion, spreading_strength, mixing, wiener):
    x_plus = padded[:, 2:]
    x_minus = padded[:, :-2]
    y_plus = jnp.roll(current, -1, 2)
    y_minus = jnp.roll(current, 1, 2)
    z_plus = jnp.roll(current, -1, 3)
    z_minus = jnp.roll(current, 1, 3)
    grad_x = 0.5 * (x_plus - x_minus)
    grad_y = 0.5 * (y_plus - y_minus)
    grad_z = 0.5 * (z_plus - z_minus)
    laplace = x_plus + x_minus + y_plus + y_minus + z_plus + z_minus - 6.0 * current
    advect = filtered_motion[0] * grad_x + filtered_motion[1] * grad_y + filtered_motion[2] * grad_z
    noise = jnp.sqrt(2.0 * spreading_strength) * (
        wiener[0] * grad_x + wiener[1] * grad_y + wiener[2] * grad_z
    )
    return current - advect + spreading_strength * laplace + noise - mixing * (current - mean)


def react(block, arrhenius, left_bilinear_weights, right_bilinear_weights, species_yield_weights):
    for substep in range(SUB):
        lowered = block.astype(jnp.bfloat16)
        forward = jnp.dot(left_bilinear_weights, lowered, preferred_element_type=jnp.float32)
        backward = jnp.dot(right_bilinear_weights, lowered, preferred_element_type=jnp.float32)
        saturation = 1.0 + forward * forward + backward * backward
        rates = (arrhenius * forward * backward / saturation).astype(jnp.bfloat16)
        block = block + chem_step * jnp.dot(
            species_yield_weights, rates, preferred_element_type=jnp.float32
        )
    return block


def kinetic_yield_term(
    carried_ensemble,
    thermal_level,
    arrhenius_prefactor,
    ignition_energy_ratio,
    left_bilinear_weights,
    right_bilinear_weights,
    species_yield_weights,
):
    species_count, planes, vertical_extent, streamwise_extent = carried_ensemble.shape

    def one_plane(plane_index, current):
        starting_ensemble = jnp.asarray(plane_index).astype(jnp.int32)
        block = lax.dynamic_slice_in_dim(current, starting_ensemble, 1, 1).reshape(
            species_count, vertical_extent * streamwise_extent
        )
        enthalpy_output = lax.dynamic_slice_in_dim(thermal_level, starting_ensemble, 1, 0).reshape(
            1, vertical_extent * streamwise_extent
        )
        arrhenius = arrhenius_prefactor[:, None] * jnp.exp(
            -ignition_energy_ratio[:, None] / enthalpy_output
        )
        reacted = react(
            block, arrhenius, left_bilinear_weights, right_bilinear_weights, species_yield_weights
        )
        reacted = reacted.reshape(species_count, 1, vertical_extent, streamwise_extent)
        return lax.dynamic_update_slice_in_dim(current, reacted, starting_ensemble, 1)

    return lax.fori_loop(0, planes, one_plane, carried_ensemble)


def body(
    composition_vector,
    filtered_motion,
    spreading_strength,
    blend_relax_multiplier,
    thermal_level,
    brownian_jumps,
    left_bilinear_weights,
    right_bilinear_weights,
    species_yield_weights,
    arrhenius_prefactor,
    ignition_energy_ratio,
):
    fields = lax.axis_size("field")
    motion_lookup, spreading_gradient_sum, subgrid_blend_sum, thermal_lookup = turned_gather(
        (filtered_motion, spreading_strength, blend_relax_multiplier, thermal_level),
        "field",
        (2, 1, 1, 1),
    )
    current = composition_vector[0]
    for step in range(STEPS):
        share = sent_and_summed(current, "field", 2) / fields
        mean = collect(share, "field", 2)
        padded = extended(current, (("space", 1),), 1)
        carried_ensemble = transport(
            padded,
            current,
            mean,
            motion_lookup,
            spreading_gradient_sum,
            subgrid_blend_sum,
            brownian_jumps[step, 0],
        )
        current = kinetic_yield_term(
            carried_ensemble,
            thermal_lookup,
            arrhenius_prefactor,
            ignition_energy_ratio,
            left_bilinear_weights,
            right_bilinear_weights,
            species_yield_weights,
        )
    return current[None]


def solution(mesh):
    return jax.shard_map(
        body,
        mesh=mesh,
        in_specs=(
            P("field", None, "space", None, None),
            P(None, "space", "field", None),
            P("space", "field", None),
            P("space", "field", None),
            P("space", "field", None),
            P(None, "field", None),
            P(),
            P(),
            P(),
            P(),
            P(),
        ),
        out_specs=P("field", None, "space", None, None),
        check_vma=False,
    )
```

profile of v0, /device:TPU:1, one launch (start us, length us, event | category | flops | bytes accessed | tf_op | source)
XLA Modules:
  0.0 204.8 jit_solution(5558131106530953683)
XLA Ops:
  0.0 2.7 %copy.133 = f32[1,32,4,16,128]{4,2,1,3,0:T(4,128)} copy(f32[1,32,4,16,128]{4,3,2,1,0:T(8,128)} %param.15) | data formatting | bytes 2097152 | tf_op args[0]
  2.7 10.3 %all-to-all-start = ((f32[16,32,4,1,128]{4,2,1,3,0:T(4,128)}), f32[16,32,4,1,128]{4,2,1,3,0:T(4,128)S(1)}, u32[]{:S(2)}, u32[]{:S(2)}) async-start(f32[16,32,4,1,128]{4,2,1,3,0:T(4,128)} %bitcast.249), calls=%async_computation | async-start | bytes 2097152 | tf_op jit(solution)/shard_map/all_to_all | solution.py:35
  14.5 9.3 %collective-permute-start = (f32[32,1,16,128]{3,0,1,2:T(8,128)}, f32[32,1,16,128]{3,0,1,2:T(8,128)}, u32[]{:S(2)}, u32[]{:S(2)}) collective-permute-start(f32[32,1,16,128]{3,0,1,2:T(8,128)} %get-tuple-element.496), channel_id=1, source_target_pairs={{16,0},{32,16},{48,32},{64,48},{80,64},{96,80},{112,96},{128,112},... | collective-permute-start | bytes 786440 | tf_op jit(solution)/shard_map/ppermute | solution.py:64
  23.8 1.9 collective-permute-start.1
  25.8 28.5 %all-gather = f32[16,1,3072]{2,1,0:T(1,128)S(1)} all-gather(f32[1,1,3072]{2,1,0:T(1,128)S(1)} %maximum_bitcast_fusion), channel_id=1, replica_groups=mesh['space'=32,'field'=16] {'field'}, dimensions={0}, use_global_device_ids=true | all-gather | bytes 208896 | tf_op jit(solution)/shard_map/all_gather | solution.py:17
  54.4 1.6 fusion.91
  56.2 1.1 broadcast_in_dim.16
  57.3 4.6 %all-to-all-start.1 = ((f32[16,32,4,1,128]{4,1,2,3,0:T(8,128)}), f32[16,32,4,1,128]{4,1,2,3,0:T(8,128)S(1)}, u32[]{:S(2)}, u32[]{:S(2)}) async-start(f32[16,32,4,1,128]{4,1,2,3,0:T(8,128)} %broadcast_in_dim.16), calls=%async_computation.1 | async-start | bytes 2097152 | tf_op jit(solution)/shard_map/all_to_all | solution.py:47
  61.9 1.4 fusion.93
  63.3 1.7 fusion.94
  67.5 11.4 %all-to-all-done.1 = f32[16,32,4,1,128]{4,1,2,3,0:T(8,128)S(1)} async-done(((f32[16,32,4,1,128]{4,1,2,3,0:T(8,128)}), f32[16,32,4,1,128]{4,1,2,3,0:T(8,128)S(1)}, u32[]{:S(2)}, u32[]{:S(2)}) %all-to-all-start.1) | async-done | bytes 1048608 | tf_op jit(solution)/shard_map/all_to_all | solution.py:47
  79.0 4.1 %fusion.81 = f32[32,4,16,128]{3,0,1,2:T(8,128)} fusion(f32[32,4,16,128]{3,0,1,2:T(8,128)S(1)} %bitcast.411, f32[16,32,4,1,128]{4,1,2,3,0:T(8,128)S(1)} %all-to-all-done.1, f32[32,4,16,127]{3,0,1,2:T(8,128)} %get-tuple-element.502, f32[32,4,16,1]{3,0,1,2:T(8,128)} %get-tuple-element.504, f32[32,4,16,1]{3,0,1,2:T(8,128)} %get-tuple-element.503, ...), kind=kLoop, calls=%fused_computation.127 | loop fusion | flops 8912896 | bytes 8060940 | tf_op jit(solution)/shard_map/sub | solution.py:84
  83.1 36.8 %while.30 = (s32[]{:T(128)}, f32[32,4,16,128]{3,0,1,2:T(8,128)}, f32[206]{0:T(256)S(1)}, f32[206,1]{0,1:T(1,128)S(1)}, f32[4,16,128]{2,1,0:T(8,128)S(1)}, /*inde...) while((s32[]{:T(128)}, f32[32,4,16,128]{3,0,1,2:T(8,128)}, ...), condition=%wide.region_2.3_spmd, body=%wide.region_1.2_spmd.sunk | while | flops 427352064 | bytes 23221052 | solution.py:128
  84.7 1.0 fusion.206
  103.1 1.0 fusion.206
  119.9 4.5 %all-to-all-start.2 = ((f32[16,32,4,1,128]{4,1,2,3,0:T(8,128)}), f32[16,32,4,1,128]{4,1,2,3,0:T(8,128)S(1)}, u32[]{:S(2)}, u32[]{:S(2)}) async-start(f32[16,32,4,1,128]{4,1,2,3,0:T(8,128)} %bitcast.59), calls=%async_computation.2 | async-start | bytes 2097152 | tf_op jit(solution)/shard_map/all_to_all | solution.py:35
  126.3 1.9 fusion.88
  128.2 13.3 %all-to-all-done.2 = f32[16,32,4,1,128]{4,1,2,3,0:T(8,128)S(1)} async-done(((f32[16,32,4,1,128]{4,1,2,3,0:T(8,128)}), f32[16,32,4,1,128]{4,1,2,3,0:T(8,128)S(1)}, u32[]{:S(2)}, u32[]{:S(2)}) %all-to-all-start.2) | async-done | bytes 1048608 | tf_op jit(solution)/shard_map/all_to_all | solution.py:35
  141.6 1.1 broadcast_in_dim.17
  142.7 4.4 %all-to-all-start.3 = ((f32[16,32,4,1,128]{4,1,2,3,0:T(8,128)}), f32[16,32,4,1,128]{4,1,2,3,0:T(8,128)S(1)}, u32[]{:S(2)}, u32[]{:S(2)}) async-start(f32[16,32,4,1,128]{4,1,2,3,0:T(8,128)} %broadcast_in_dim.17), calls=%async_computation.3 | async-start | bytes 2097152 | tf_op jit(solution)/shard_map/all_to_all | solution.py:47
  147.2 1.1 fusion.85
  148.2 9.3 %collective-permute-start.2 = (f32[32,1,16,128]{3,0,1,2:T(8,128)S(1)}, f32[32,1,16,128]{3,0,1,2:T(8,128)S(1)}, u32[]{:S(2)}, u32[]{:S(2)}) collective-permute-start(f32[32,1,16,128]{3,0,1,2:T(8,128)S(1)} %get-tuple-element.486), channel_id=1, source_target_pairs={{16,0},{32,16},{48,32},{64,48},{80,64},{96,80},{112,96},{128,112},... | collective-permute-start | bytes 786440 | tf_op jit(solution)/shard_map/ppermute | solution.py:64
  157.6 2.1 %collective-permute-start.3 = (f32[32,1,16,128]{3,0,1,2:T(8,128)S(1)}, f32[32,1,16,128]{3,0,1,2:T(8,128)}, u32[]{:S(2)}, u32[]{:S(2)}) collective-permute-start(f32[32,1,16,128]{3,0,1,2:T(8,128)S(1)} %get-tuple-element.485), channel_id=1, source_target_pairs={{0,16},{16,32},{32,48},{48,64},{64,80},{80,96},{96,112},{112,128},... | collective-permute-start | bytes 786440 | tf_op jit(solution)/shard_map/ppermute | solution.py:63
  159.7 3.3 %fusion.89 = (f32[32,4,16,1]{3,0,1,2:T(8,128)}, f32[32,4,16,1]{3,0,1,2:T(8,128)}) fusion(f32[32,4,16,128]{3,0,1,2:T(8,128)} %get-tuple-element.387), kind=kLoop, calls=%fused_computation.145 | loop fusion | bytes 32768 | tf_op jit(solution)/shard_map/jit(_roll_static)/slice | solution.py:74
  163.0 3.1 %fusion.86 = (f32[32,4,15,128]{3,0,1,2:T(8,128)}, f32[32,4,15,128]{3,0,1,2:T(8,128)}) fusion(f32[32,4,16,128]{3,0,1,2:T(8,128)} %get-tuple-element.387), kind=kLoop, calls=%fused_computation.142 | loop fusion | bytes 3932160 | tf_op jit(solution)/shard_map/jit(_roll_static)/slice | solution.py:72
  167.7 2.4 %collective-permute-done.3 = f32[32,1,16,128]{3,0,1,2:T(8,128)} collective-permute-done((f32[32,1,16,128]{3,0,1,2:T(8,128)S(1)}, f32[32,1,16,128]{3,0,1,2:T(8,128)}, u32[]{:S(2)}, u32[]{:S(2)}) %collective-permute-start.3) | collective-permute-done | bytes 262176 | tf_op jit(solution)/shard_map/ppermute | solution.py:63
  170.1 3.8 %fusion.79 = f32[32,4,16,128]{3,0,1,2:T(8,128)S(1)} fusion(f32[32,4,16,128]{3,0,1,2:T(8,128)} %get-tuple-element.387, f32[16,32,4,1,128]{4,1,2,3,0:T(8,128)S(1)} %all-to-all-done.3, f32[32,4,16,127]{3,0,1,2:T(8,128)S(1)} %get-tuple-element.492, f32[32,4,16,1]{3,0,1,2:T(8,128)} %get-tuple-element.494, f32[32,4,16,1]{3,0,1,2:T(8,128)} %get-tuple-element.493, ...), kind=kLoop, calls=%fused_computation.124 | loop fusion | flops 8912896 | bytes 8060940 | tf_op jit(solution)/shard_map/sub | solution.py:84
  174.6 29.3 %while.31 = (s32[]{:T(128)}, f32[32,4,16,128]{3,2,1,0:T(8,128)S(1)}, f32[206]{0:T(256)S(1)}, f32[206,1]{0,1:T(1,128)S(1)}, f32[4,16,128]{2,1,0:T(8,128)S(1)}, /*...) while((s32[]{:T(128)}, ...), condition=%wide.region_5.6_spmd, body=%wide.region_4.5_spmd.sunk | while | flops 427352064 | bytes 22644000 | solution.py:128
  175.0 1.0 fusion.234
  182.4 1.0 fusion.234
  189.7 1.0 fusion.234
  197.0 1.0 fusion.234
  (171 shorter events, 65.0 us)
Async XLA Ops:
  0.0 13.0 %copy-start.2 = (f32[1,32,4,16,128]{4,3,2,1,0:T(8,128)S(1)}, f32[1,32,4,16,128]{4,3,2,1,0:T(8,128)}, u32[]{:S(2)}) copy-start(f32[1,32,4,16,128]{4,3,2,1,0:T(8,128)} %param.15) | copy-start | bytes 3145732
  2.7 53.3 %all-to-all-start = ((f32[16,32,4,1,128]{4,2,1,3,0:T(4,128)}), f32[16,32,4,1,128]{4,2,1,3,0:T(4,128)S(1)}, u32[]{:S(2)}, u32[]{:S(2)}) async-start(f32[16,32,4,1,128]{4,2,1,3,0:T(4,128)} %bitcast.249), calls=%async_computation | async-start | bytes 2097152 | tf_op jit(solution)/shard_map/all_to_all | solution.py:35
  13.0 12.7 %copy-start.5 = (f32[3,4,1,128]{3,2,1,0:T(1,128)S(1)}, f32[3,4,1,128]{3,2,1,0:T(1,128)}, u32[]{:S(2)}) copy-start(f32[3,4,1,128]{3,2,1,0:T(1,128)} %param.16) | copy-start | bytes 18436
  13.0 12.7 %copy-start.6 = (f32[4,1,128]{2,1,0:T(1,128)S(1)}, f32[4,1,128]{2,1,0:T(1,128)}, u32[]{:S(2)}) copy-start(f32[4,1,128]{2,1,0:T(1,128)} %param.19) | copy-start | bytes 6148
  13.0 12.7 %copy-start.7 = (f32[4,1,128]{2,1,0:T(1,128)S(1)}, f32[4,1,128]{2,1,0:T(1,128)}, u32[]{:S(2)}) copy-start(f32[4,1,128]{2,1,0:T(1,128)} %param.18) | copy-start | bytes 6148
  13.0 12.7 %copy-start.8 = (f32[4,1,128]{2,1,0:T(1,128)S(1)}, f32[4,1,128]{2,1,0:T(1,128)}, u32[]{:S(2)}) copy-start(f32[4,1,128]{2,1,0:T(1,128)} %param.17) | copy-start | bytes 6148
  14.5 53.0 %collective-permute-start = (f32[32,1,16,128]{3,0,1,2:T(8,128)}, f32[32,1,16,128]{3,0,1,2:T(8,128)}, u32[]{:S(2)}, u32[]{:S(2)}) collective-permute-start(f32[32,1,16,128]{3,0,1,2:T(8,128)} %get-tuple-element.496), channel_id=1, source_target_pairs={{16,0},{32,16},{48,32},{64,48},{80,64},{96,80},{112,96},{128,112},... | collective-permute-start | bytes 786440 | tf_op jit(solution)/shard_map/ppermute | solution.py:64
  23.8 43.7 %collective-permute-start.1 = (f32[32,1,16,128]{3,0,1,2:T(8,128)}, f32[32,1,16,128]{3,0,1,2:T(8,128)}, u32[]{:S(2)}, u32[]{:S(2)}) collective-permute-start(f32[32,1,16,128]{3,0,1,2:T(8,128)} %get-tuple-element.495), channel_id=1, source_target_pairs={{0,16},{16,32},{32,48},{48,64},{64,80},{80,96},{96,112},{112,128},... | collective-permute-start | bytes 786440 | tf_op jit(solution)/shard_map/ppermute | solution.py:63
  57.3 21.7 %all-to-all-start.1 = ((f32[16,32,4,1,128]{4,1,2,3,0:T(8,128)}), f32[16,32,4,1,128]{4,1,2,3,0:T(8,128)S(1)}, u32[]{:S(2)}, u32[]{:S(2)}) async-start(f32[16,32,4,1,128]{4,1,2,3,0:T(8,128)} %broadcast_in_dim.16), calls=%async_computation.1 | async-start | bytes 2097152 | tf_op jit(solution)/shard_map/all_to_all | solution.py:47
  63.3 1.7 copy-start.4
  63.3 4.2 %copy-start.9 = (f32[206]{0:T(256)S(1)}, f32[206]{0:T(256)}, u32[]{:S(2)}) copy-start(f32[206]{0:T(256)} %param.25) | copy-start | bytes 2476
  79.0 4.1 %copy-start = (bf16[206,32]{0,1:T(8,128)(2,1)S(1)}, bf16[206,32]{0,1:T(8,128)(2,1)}, u32[]{:S(2)}) copy-start(bf16[206,32]{0,1:T(8,128)(2,1)} %param.21) | copy-start | bytes 39556
  79.0 4.1 %copy-start.10 = (bf16[206,32]{0,1:T(8,128)(2,1)S(1)}, bf16[206,32]{0,1:T(8,128)(2,1)}, u32[]{:S(2)}) copy-start(bf16[206,32]{0,1:T(8,128)(2,1)} %param.22) | copy-start | bytes 39556
  79.0 4.1 %copy-start.13 = (f32[206]{0:T(256)S(1)}, f32[206]{0:T(256)}, u32[]{:S(2)}) copy-start(f32[206]{0:T(256)} %param.24) | copy-start | bytes 2476
  83.1 1.6 copy-start.11
  92.3 1.6 copy-start.11
  101.5 1.6 copy-start.11
  110.7 1.6 copy-start.11
  119.9 21.6 %all-to-all-start.2 = ((f32[16,32,4,1,128]{4,1,2,3,0:T(8,128)}), f32[16,32,4,1,128]{4,1,2,3,0:T(8,128)S(1)}, u32[]{:S(2)}, u32[]{:S(2)}) async-start(f32[16,32,4,1,128]{4,1,2,3,0:T(8,128)} %bitcast.59), calls=%async_computation.2 | async-start | bytes 2097152 | tf_op jit(solution)/shard_map/all_to_all | solution.py:35
  142.7 27.3 %all-to-all-start.3 = ((f32[16,32,4,1,128]{4,1,2,3,0:T(8,128)}), f32[16,32,4,1,128]{4,1,2,3,0:T(8,128)S(1)}, u32[]{:S(2)}, u32[]{:S(2)}) async-start(f32[16,32,4,1,128]{4,1,2,3,0:T(8,128)} %broadcast_in_dim.17), calls=%async_computation.3 | async-start | bytes 2097152 | tf_op jit(solution)/shard_map/all_to_all | solution.py:47
  148.2 18.7 %collective-permute-start.2 = (f32[32,1,16,128]{3,0,1,2:T(8,128)S(1)}, f32[32,1,16,128]{3,0,1,2:T(8,128)S(1)}, u32[]{:S(2)}, u32[]{:S(2)}) collective-permute-start(f32[32,1,16,128]{3,0,1,2:T(8,128)S(1)} %get-tuple-element.486), channel_id=1, source_target_pairs={{16,0},{32,16},{48,32},{64,48},{80,64},{96,80},{112,96},{128,112},... | collective-permute-start | bytes 786440 | tf_op jit(solution)/shard_map/ppermute | solution.py:64
  157.6 12.5 %collective-permute-start.3 = (f32[32,1,16,128]{3,0,1,2:T(8,128)S(1)}, f32[32,1,16,128]{3,0,1,2:T(8,128)}, u32[]{:S(2)}, u32[]{:S(2)}) collective-permute-start(f32[32,1,16,128]{3,0,1,2:T(8,128)S(1)} %get-tuple-element.485), channel_id=1, source_target_pairs={{0,16},{16,32},{32,48},{48,64},{64,80},{80,96},{96,112},{112,128},... | collective-permute-start | bytes 786440 | tf_op jit(solution)/shard_map/ppermute | solution.py:63
  166.9 0.7 copy-start.3
  173.8 0.7 copy-start.12
  203.8 1.0 copy-start.1
where the time goes:
time: 206 us; the launch traced here: 205 us
  matrix products  56.8 us (28%)
  starting transfers between devices  46.5 us (23%)
  local copies, waits for them, and re-layouts  32.8 us (16%)
  blocking collectives  28.5 us (14%)
  waiting for transfers between devices  27.2 us (13%)
  other arithmetic  8.22 us (4%)
  between operations  4.06 us (2%)
    dot_general x40, matrix products, react(): jnp.dot(species_yield_weights, rates, preferred_element_type=jnp.float32)  40.1 us
    all_gather x1, blocking collectives, turned_gather(): result = lax.all_gather(both, axis, axis=0, tiled=True)  28.5 us
    ppermute x2, starting transfers between devices, extended(): after = lax.ppermute(leading, axis, down)  18.6 us
    dot_general x40, matrix products, react(): jnp.dot(left_bilinear_weights, lowered, preferred_element_type=jnp.float32)  16.6 us
    all_to_all x2, starting transfers between devices, sent_and_summed(): lax.all_to_all(tiles, axis, split_axis=0, concat_axis=0, tiled=True)  14.7 us
    all_to_all x2, waiting for transfers between devices, sent_and_summed(): lax.all_to_all(tiles, axis, split_axis=0, concat_axis=0, tiled=True)  13.3 us
    all_to_all x2, waiting for transfers between devices, from_everyone(): lax.all_to_all(jnp.broadcast_to(value[None], (count, *value.shape)), axis...  11.4 us
    all_to_all x2, starting transfers between devices, from_everyone(): lax.all_to_all(jnp.broadcast_to(value[None], (count, *value.shape)), axis...  9.09 us
  transfers between devices with their start and end apart: 8, of which 3 were waited for; matrix products, arithmetic and copies ran while one was open for 9% of the time, Pallas kernels for 0%

commit v1 on v0

v1 whole, which is shorter than its diff:
```python
import functools

import jax
import jax.numpy as jnp
from jax import lax
from jax.experimental import pallas as pl
from jax.experimental.pallas import tpu as pltpu
from jax.sharding import PartitionSpec as P

STEPS = 2
SUB = 5
CHEM_STEP = 0.2
F32, BF16 = jnp.float32, jnp.bfloat16
LANES = 128
VMEM = pl.BlockSpec(memory_space=pltpu.VMEM)


def lane_index(rows):
    return lax.broadcasted_iota(jnp.int32, (rows, LANES), 1)


def turn(x, shift):
    shift %= LANES
    return x if shift == 0 else pltpu.roll(x, shift, 1)


def swap_chunks(tiles, chunk):
    count = len(tiles)
    place = lane_index(tiles[0].shape[0]) // chunk
    step = 1
    while step < count:
        upper = (place // step) % 2 == 1
        fresh = list(tiles)
        for a in range(count):
            if (a // step) % 2 == 0:
                b = a + step
                fresh[a] = jnp.where(upper, turn(tiles[b], step * chunk), tiles[a])
                fresh[b] = jnp.where(upper, tiles[b], turn(tiles[a], -step * chunk))
        tiles = fresh
        step *= 2
    return tiles


def pack_kernel(cur, motion, spread, mix, therm, jumps, out):
    planes, rows, species, _ = cur.shape
    parts, chunk = rows, LANES // rows

    def one(i, _):
        x, g = i // (species // 8), i % (species // 8)
        at = pl.ds(pl.multiple_of(g * 8, 8), 8)
        tiles = swap_chunks([cur[x, y, at, :] for y in range(rows)], chunk)
        to = pl.ds(pl.multiple_of(x * species + g * 8, 8), 8)
        for j in range(parts):
            out[j, to, :] = tiles[j]
        return 0

    lax.fori_loop(0, planes * (species // 8), one, 0)
    lines = [motion[c, x] for c in range(3) for x in range(planes)]
    lines += [ref[x] for ref in (spread, mix, therm) for x in range(planes)]
    blocks = [jnp.concatenate(lines[8 * a : 8 * a + 8], axis=0) for a in range(3)]
    place = lane_index(8) // chunk
    line = lax.broadcasted_iota(jnp.int32, (8, LANES), 0)
    noise = jnp.zeros((8, LANES), F32)
    for r in range(3 * STEPS):
        noise = jnp.where(line == r, jumps[r // 3, 0, r % 3], noise)
    for j in range(parts):
        packed = jnp.where(place == 3, noise, turn(blocks[0], -chunk * j))
        for a in (1, 2):
            packed = jnp.where(place == a, turn(blocks[a], chunk * (a - j)), packed)
        out[j, planes * species :, :] = packed


def pack_z(read, low, high, fields, species, pairs):
    spot = lane_index(species) % 8
    for p, pair in enumerate(pairs):
        for g in range(fields // 4):
            first = last = None
            for k in range(8):
                tile = read(4 * g + k % 4, pair[k // 4])
                lo, hi = turn(tile, k), turn(tile, k - 7)
                first = lo if first is None else jnp.where(spot == k, lo, first)
                last = hi if last is None else jnp.where(spot == k, hi, last)
            low[p * (fields // 4) + g] = first
            high[p * (fields // 4) + g] = last


PAIRS = ((1, 2), (0, 3))


def open_kernel(planes, species, got, x_low, x_high, z_low, z_high, flow, wiener):
    fields = got.shape[0]
    chunk = LANES // fields
    read = lambda f, x: got[f, x * species : (x + 1) * species, :]
    for f in range(fields):
        x_low[f] = read(f, 0)
        x_high[f] = read(f, planes - 1)
    pack_z(read, z_low, z_high, fields, species, PAIRS)
    place = lane_index(8) // chunk
    for a in range(3):
        block = None
        for y in range(fields):
            piece = turn(got[y, planes * species :, :], chunk * (y - a))
            block = piece if block is None else jnp.where(place == y, piece, block)
        flow[8 * a : 8 * a + 8, :] = block
    for f in range(fields):
        noise = got[f, planes * species :, 3 * chunk : 3 * chunk + 1]
        wiener[f] = jnp.broadcast_to(noise, (8, LANES))


def step_kernel(step, halos, cur, before, after, z_after, z_before, flow, wiener, kinetics, left, right, gain, *rest):
    outs, (padded, means, arr, w, y) = rest[: 5 if halos else 1], rest[5 if halos else 1 :]
    out = outs[0]
    fields, species = before.shape[0], before.shape[1]
    planes = 4
    reactions = left.shape[0]
    ceil = w.shape[0] // 2
    w[...] = jnp.zeros_like(w)
    w[0:reactions, :] = left[...]
    w[ceil : ceil + reactions, :] = right[...]
    y[...] = jnp.zeros_like(y)
    y[:, 0:reactions] = gain[...]
    for f in range(fields):
        padded[0, f] = before[f]
        padded[planes + 1, f] = after[f]
        for x in range(planes):
            padded[x + 1, f] = cur[f, x * species : (x + 1) * species, :]
    spot = lane_index(species) % 8
    pre, energy = kinetics[:, 0:1], kinetics[:, 1:2]

    def plane(x, _):
        row = lambda c: flow[pl.ds(c * planes + x, 1), :]
        u = [row(0), row(1), row(2)]
        diffusion, mixing, heat = row(3), row(4), row(5)
        arr[...] = pre * jnp.exp(-energy / heat)
        total = padded[x + 1, 0]
        for f in range(1, fields):
            total = total + padded[x + 1, f]
        means[...] = (mixing * (1.0 / fields)) * total
        root = jnp.sqrt(2.0 * diffusion)
        inner = (x == 1) | (x == 2)
        pair = jnp.where(inner, 0, fields // 4)
        second = x >= 2
        centre = 1.0 - 6.0 * diffusion - mixing
        blocks = []
        for f in range(fields):
            here = padded[x + 1, f]
            sign = [0.5 * (root * wiener[f, 3 * step + d : 3 * step + d + 1, :] - u[d]) for d in range(3)]
            plus = [diffusion + s for s in sign]
            minus = [diffusion - s for s in sign]
            k = f % 4
            edge_after = z_after[pair + f // 4]
            edge_before = z_before[pair + f // 4]
            edge_after = jnp.where(second, turn(edge_after, 3 - k), turn(edge_after, 7 - k))
            edge_before = jnp.where(second, turn(edge_before, -4 - k), turn(edge_before, -k))
            z_plus = jnp.where(spot == 7, edge_after, turn(here, -1))
            z_minus = jnp.where(spot == 0, edge_before, turn(here, 1))
            moved = centre * here + means[...]
            moved = moved + plus[0] * padded[x + 2, f] + minus[0] * padded[x, f]
            moved = moved + plus[1] * turn(here, -8) + minus[1] * turn(here, 8)
            moved = moved + plus[2] * z_plus + minus[2] * z_minus
            blocks.append(moved)
        block = jnp.concatenate(blocks, axis=1)
        factor = jnp.concatenate([arr[...]] * fields, axis=1)
        for _ in range(SUB):
            low = block.astype(BF16)
            both = jnp.dot(w[...], low, preferred_element_type=F32)
            f, b = both[:ceil], both[ceil:]
            rates = (factor * f * b / (1.0 + f * f + b * b)).astype(BF16)
            block = block + CHEM_STEP * jnp.dot(y[...], rates, preferred_element_type=F32)
        to = pl.ds(pl.multiple_of(x * species, species), species)
        for f in range(fields):
            out[f, to, :] = block[:, f * LANES : (f + 1) * LANES]
        return 0

    lax.fori_loop(0, planes, plane, 0)
    if halos:
        x_low, x_high, z_low, z_high = outs[1:]
        read = lambda f, x: out[f, x * species : (x + 1) * species, :]
        for f in range(fields):
            x_low[f] = read(f, 0)
            x_high[f] = read(f, planes - 1)
        pack_z(read, z_low, z_high, fields, species, PAIRS)


def close_kernel(got, out):
    planes, rows, species, _ = out.shape
    chunk = LANES // rows

    def one(i, _):
        x, g = i // (species // 8), i % (species // 8)
        start = pl.ds(pl.multiple_of(x * species + g * 8, 8), 8)
        tiles = swap_chunks([got[j, start, :] for j in range(rows)], chunk)
        at = pl.ds(pl.multiple_of(g * 8, 8), 8)
        for y in range(rows):
            out[x, y, at, :] = tiles[y]
        return 0

    lax.fori_loop(0, planes * (species // 8), one, 0)


def shape(*dims):
    return jax.ShapeDtypeStruct(dims, F32)


def call(kernel, outs, ins, scratch=(), name=None, cost=None):
    return pl.pallas_call(
        kernel,
        out_shape=outs,
        in_specs=ins,
        out_specs=[VMEM] * len(outs) if isinstance(outs, (list, tuple)) else VMEM,
        scratch_shapes=list(scratch),
        name=name,
        cost_estimate=cost,
        compiler_params=pltpu.CompilerParams(vmem_limit_bytes=40 << 20),
    )


def neighbours(value_up, value_down, axis):
    count = lax.axis_size(axis)
    up = [(i, (i + 1) % count) for i in range(count)]
    down = [(j, i) for i, j in up]
    return lax.ppermute(value_up, axis, up), lax.ppermute(value_down, axis, down)


def body(comp, motion, spread, mix, therm, jumps, left, right, gain, prefactor, energy):
    fields = lax.axis_size("field")
    _, species, planes, rows, lanes = comp.shape
    reactions = left.shape[0]
    ceil = -(-reactions // 16) * 16
    cells = planes * species
    turned = comp[0].transpose(1, 2, 0, 3)
    sent = call(pack_kernel, shape(fields, cells + 8, lanes), [VMEM] * 5 + [pl.BlockSpec(memory_space=pltpu.SMEM)], name="pack")(
        turned, motion, spread, mix, therm, jumps
    )
    kinetics = jnp.pad(jnp.stack([prefactor, energy], 1), ((0, ceil - reactions), (0, 0)))
    cur = lax.all_to_all(sent, "field", 0, 0, tiled=True)
    edge = [shape(fields, species, lanes)] * 2 + [shape(fields // 2, species, lanes)] * 2
    *edges, flow, wiener = call(
        functools.partial(open_kernel, planes, species),
        edge + [shape(24, lanes), shape(fields, 8, lanes)],
        [VMEM],
        name="open",
    )(cur)
    flops = 2 * SUB * fields * planes * lanes * 3 * ceil * species
    for step in range(STEPS):
        before, after = neighbours(edges[1], edges[0], "space")
        z_before, z_after = neighbours(edges[3], edges[2], "field")
        last = step == STEPS - 1
        cur, *edges = call(
            functools.partial(step_kernel, step, not last),
            [shape(fields, cells, lanes)] + ([] if last else edge),
            [VMEM] * 11,
            scratch=[
                pltpu.VMEM((planes + 2, fields, species, lanes), F32),
                pltpu.VMEM((species, lanes), F32),
                pltpu.VMEM((ceil, lanes), F32),
                pltpu.VMEM((2 * ceil, species), BF16),
                pltpu.VMEM((species, ceil), BF16),
            ],
            name=f"step{step}",
            cost=pl.CostEstimate(flops=flops, bytes_accessed=4 << 20, transcendentals=0),
        )(cur, before, after, z_after, z_before, flow, wiener, kinetics, left, right, gain)
    got = lax.all_to_all(cur, "field", 0, 0, tiled=True)
    done = call(close_kernel, shape(planes, rows, species, lanes), [VMEM], name="close")(got)
    return done.transpose(2, 0, 1, 3)[None]


def solution(mesh):
    return jax.shard_map(
        body,
        mesh=mesh,
        in_specs=(
            P("field", None, "space", None, None),
            P(None, "space", "field", None),
            P("space", "field", None),
            P("space", "field", None),
            P("space", "field", None),
            P(None, "field", None),
            P(),
            P(),
            P(),
            P(),
            P(),
        ),
        out_specs=P("field", None, "space", None, None),
        check_vma=False,
    )
```

time: 206 us -> 145 us (0.70)
  matrix products: 56.8 us -> 0 us
  Pallas kernels: 0 us -> 47 us
  local copies, waits for them, and re-layouts: 32.8 us -> 3.87 us
  blocking collectives: 28.5 us -> 54.1 us
  waiting for transfers between devices: 27.2 us -> 4.14 us
  starting transfers between devices: 46.5 us -> 35.6 us
  other arithmetic: 8.22 us -> 0.01 us
  between operations: 4.06 us -> 0.24 us
    dot_general x80 -> x0, matrix products: 56.8 us -> none  [the longest x40 40.1 us: react(): jnp.dot(species_yield_weights, rates, preferred_element_type=jnp.float32)]
    all_to_all x0 -> x2, blocking collectives: none -> 54.1 us  [the longest x1 27.7 us: body(): cur = lax.all_to_all(sent, 'field', 0, 0, tiled=True)]
    pallas_call x0 -> x5, Pallas kernels: none -> 47 us  [the longest x2 35.8 us: body(): call(functools.partial(step_kernel, step, not last), [shape(fields, cells...]
    all_gather x1 -> x0, blocking collectives: 28.5 us -> none  [turned_gather(): result = lax.all_gather(both, axis, axis=0, tiled=True)]
    all_to_all x4 -> x0, waiting for transfers between devices: 24.8 us -> none  [the longest x2 13.3 us: sent_and_summed(): lax.all_to_all(tiles, axis, split_axis=0, concat_axis=0, tiled=True)]
    all_to_all x4 -> x0, starting transfers between devices: 23.8 us -> none  [the longest x2 14.7 us: sent_and_summed(): lax.all_to_all(tiles, axis, split_axis=0, concat_axis=0, tiled=True)]
    slice x11 -> x0, local copies, waits for them, and re-layouts: 16.3 us -> none  [the longest x4 8.21 us: transport(): z_plus = jnp.roll(current, -1, 3)]
    ppermute x4 -> x8, starting transfers between devices: 22.7 us -> 35.6 us  [the longest x4 26.9 us: neighbours(): lax.ppermute(value_down, axis, down)]
  transfers between devices with their start and end apart: 8 -> 8, of which waited for: 3 -> 3; matrix products, arithmetic and copies ran while one was open for 9% -> 0% of each run, Pallas kernels for 0% -> 0%
where the time goes in v1:
time: 145 us
  blocking collectives  54.1 us (37%)
  Pallas kernels  47 us (32%)
  starting transfers between devices  35.6 us (25%)
  waiting for transfers between devices  4.14 us (3%)
  local copies, waits for them, and re-layouts  3.87 us (3%)
    pallas_call x2, Pallas kernels, body(): call(functools.partial(step_kernel, step, not last), [shape(fields, cells...  35.8 us
    all_to_all x1, blocking collectives, body(): cur = lax.all_to_all(sent, 'field', 0, 0, tiled=True)  27.7 us
    ppermute x4, starting transfers between devices, neighbours(): lax.ppermute(value_down, axis, down)  26.9 us
    all_to_all x1, blocking collectives, body(): got = lax.all_to_all(cur, 'field', 0, 0, tiled=True)  26.5 us
    ppermute x4, starting transfers between devices, neighbours(): lax.ppermute(value_up, axis, up)  8.7 us
    pallas_call x1, Pallas kernels, body(): call(pack_kernel, shape(fields, cells + 8, lanes), [VMEM] * 5 + [pl.Block...  5.63 us
    pallas_call x1, Pallas kernels, body(): call(close_kernel, shape(planes, rows, species, lanes), [VMEM], name='clo...  4.96 us
    ppermute x4, waiting for transfers between devices, neighbours(): lax.ppermute(value_up, axis, up)  3.85 us
  transfers between devices with their start and end apart: 8, of which 3 were waited for; matrix products, arithmetic and copies ran while one was open for 0% of the time, Pallas kernels for 0%

profile of v1, /device:TPU:1, one launch (start us, length us, event | category | flops | bytes accessed | tf_op | source)
XLA Modules:
  0.0 145.0 jit_solution(15858529089420701905)
XLA Ops:
  0.0 1.9 %copy.34 = f32[1,32,4,16,128]{4,1,3,2,0:T(8,128)S(1)} copy(f32[1,32,4,16,128]{4,3,2,1,0:T(8,128)} %param.11) | data formatting | bytes 2097152 | tf_op args[0]
  1.9 0.0 copy-done.4
  1.9 0.0 copy-done.3
  1.9 0.0 copy-done.2
  2.0 5.6 %pack.1 = f32[16,136,128]{2,1,0:T(8,128)S(1)} custom-call(f32[4,16,32,128]{3,2,1,0:T(8,128)S(1)} %bitcast.11, f32[3,4,1,128]{3,2,1,0:T(1,128)S(1)} %copy-done, f32[4,1,128]{2,1,0:T(1,128)S(1)} %copy-done.1, f32[4,1,128]{2,1,0:T(1,128)S(1)} %copy-done.2, f32[4,1,128]{2,1,0:T(1,128)S(1)} %copy-done.3, f32[2,1,3]{2,1,0:T(1,128)S(1)} %copy-done.4), custom_call_target="tpu_custom_call" | custom-call | tf_op jit(solution)/shard_map/pack/pallas_call | solution.py:232
  7.6 27.7 %all_to_all.10.got.cur = f32[16,136,128]{2,1,0:T(8,128)S(1)} all-to-all(f32[16,136,128]{2,1,0:T(8,128)S(1)} %pack.1), channel_id=1, replica_groups=mesh['space'=32,'field'=16] {'field'}, dimensions={0} | all-to-all | bytes 2228224 | tf_op jit(solution)/shard_map/all_to_all | solution.py:236
  35.3 0.0 copy-start.5
  35.3 0.6 open.1
  35.9 1.9 %collective-permute-start = (f32[16,32,128]{2,1,0:T(8,128)S(1)}, f32[16,32,128]{2,1,0:T(8,128)S(1)}, u32[]{:S(2)}, u32[]{:S(2)}) collective-permute-start(f32[16,32,128]{2,1,0:T(8,128)S(1)} %get-tuple-element.16), channel_id=1, source_target_pairs={{0,16},{16,32},{32,48},{48,64},{64,80},{80,96},{96,112},{112,128},... | collective-permute-start | bytes 786440 | tf_op jit(solution)/shard_map/ppermute | solution.py:222
  37.8 10.1 %collective-permute-start.1 = (f32[16,32,128]{2,1,0:T(8,128)S(1)}, f32[16,32,128]{2,1,0:T(8,128)S(1)}, u32[]{:S(2)}, u32[]{:S(2)}) collective-permute-start(f32[16,32,128]{2,1,0:T(8,128)S(1)} %get-tuple-element.17), channel_id=1, source_target_pairs={{16,0},{32,16},{48,32},{64,48},{80,64},{96,80},{112,96},{128,112},... | collective-permute-start | bytes 786440 | tf_op jit(solution)/shard_map/ppermute | solution.py:222
  47.9 2.6 %collective-permute-start.2 = (f32[8,32,128]{2,1,0:T(8,128)S(1)}, f32[8,32,128]{2,1,0:T(8,128)S(1)}, u32[]{:S(2)}, u32[]{:S(2)}) collective-permute-start(f32[8,32,128]{2,1,0:T(8,128)S(1)} %get-tuple-element.18), channel_id=1, source_target_pairs={{1,0},{2,1},{3,2},{4,3},{5,4},{6,5},{7,6},{8,7},{9,8},{10,9},{11,1... | collective-permute-start | bytes 393224 | tf_op jit(solution)/shard_map/ppermute | solution.py:222
  50.5 2.9 %collective-permute-start.3 = (f32[8,32,128]{2,1,0:T(8,128)S(1)}, f32[8,32,128]{2,1,0:T(8,128)S(1)}, u32[]{:S(2)}, u32[]{:S(2)}) collective-permute-start(f32[8,32,128]{2,1,0:T(8,128)S(1)} %get-tuple-element.19), channel_id=1, source_target_pairs={{0,1},{1,2},{2,3},{3,4},{4,5},{5,6},{6,7},{7,8},{8,9},{9,10},{10,1... | collective-permute-start | bytes 393224 | tf_op jit(solution)/shard_map/ppermute | solution.py:222
  53.5 0.1 copy.28.left
  53.6 0.1 copy.29.right
  53.7 0.1 copy.27
  53.9 0.3 collective-permute-done.2.z_after
  54.2 1.2 collective-permute-done.3.z_before
  55.4 0.0 collective-permute-done.before
  55.4 0.0 collective-permute-done.1.after
  55.4 18.1 %step0.1 = (f32[16,128,128]{2,1,0:T(8,128)S(1)}, f32[16,32,128]{2,1,0:T(8,128)S(1)}, f32[16,32,128]{2,1,0:T(8,128)S(1)}, f32[8,32,128]{2,1,0:T(8,128)S(1)}, f32[8,32,128]{2,1,0:T(8,128)S(1)}) custom-call(f32[16,136,128]{2,1,0:T(8,128)S(1)} %all_to_all.10.got.cur, f32[16,32,128]{2,1,0:T(8,128)S(1)} %collective-permute-done.before, ...), custom_call_target="tpu_custom_call" | custom-call | flops 1635778560 | bytes 4194304 | tf_op jit(solution)/shard_map/step0/pallas_call | solution.py:249
  73.5 1.9 %collective-permute-start.4 = (f32[16,32,128]{2,1,0:T(8,128)S(1)}, f32[16,32,128]{2,1,0:T(8,128)S(1)}, u32[]{:S(2)}, u32[]{:S(2)}) collective-permute-start(f32[16,32,128]{2,1,0:T(8,128)S(1)} %get-tuple-element.23), channel_id=1, source_target_pairs={{0,16},{16,32},{32,48},{48,64},{64,80},{80,96},{96,112},{112,128},... | collective-permute-start | bytes 786440 | tf_op jit(solution)/shard_map/ppermute | solution.py:222
  75.5 6.1 %collective-permute-start.5 = (f32[16,32,128]{2,1,0:T(8,128)S(1)}, f32[16,32,128]{2,1,0:T(8,128)S(1)}, u32[]{:S(2)}, u32[]{:S(2)}) collective-permute-start(f32[16,32,128]{2,1,0:T(8,128)S(1)} %get-tuple-element.24), channel_id=1, source_target_pairs={{16,0},{32,16},{48,32},{64,48},{80,64},{96,80},{112,96},{128,112},... | collective-permute-start | bytes 786440 | tf_op jit(solution)/shard_map/ppermute | solution.py:222
  81.6 8.1 %collective-permute-start.6 = (f32[8,32,128]{2,1,0:T(8,128)S(1)}, f32[8,32,128]{2,1,0:T(8,128)S(1)}, u32[]{:S(2)}, u32[]{:S(2)}) collective-permute-start(f32[8,32,128]{2,1,0:T(8,128)S(1)} %get-tuple-element.25), channel_id=1, source_target_pairs={{1,0},{2,1},{3,2},{4,3},{5,4},{6,5},{7,6},{8,7},{9,8},{10,9},{11,1... | collective-permute-start | bytes 393224 | tf_op jit(solution)/shard_map/ppermute | solution.py:222
  89.7 1.9 %collective-permute-start.7 = (f32[8,32,128]{2,1,0:T(8,128)S(1)}, f32[8,32,128]{2,1,0:T(8,128)S(1)}, u32[]{:S(2)}, u32[]{:S(2)}) collective-permute-start(f32[8,32,128]{2,1,0:T(8,128)S(1)} %get-tuple-element.26), channel_id=1, source_target_pairs={{0,1},{1,2},{2,3},{3,4},{4,5},{5,6},{6,7},{7,8},{8,9},{9,10},{10,1... | collective-permute-start | bytes 393224 | tf_op jit(solution)/shard_map/ppermute | solution.py:222
  91.7 0.0 collective-permute-done.6.z_after
  91.7 2.6 %collective-permute-done.7.z_before = f32[8,32,128]{2,1,0:T(8,128)S(1)} collective-permute-done((f32[8,32,128]{2,1,0:T(8,128)S(1)}, f32[8,32,128]{2,1,0:T(8,128)S(1)}, u32[]{:S(2)}, u32[]{:S(2)}) %collective-permute-start.7) | collective-permute-done | bytes 131104 | tf_op jit(solution)/shard_map/ppermute | solution.py:222
  94.3 0.0 collective-permute-done.4.before
  94.3 0.0 collective-permute-done.5.after
  94.3 17.6 %step1.1 = f32[16,128,128]{2,1,0:T(8,128)S(1)} custom-call(f32[16,128,128]{2,1,0:T(8,128)S(1)} %get-tuple-element.22.cur, f32[16,32,128]{2,1,0:T(8,128)S(1)} %collective-permute-done.4.before, f32[16,32,128]{2,1,0:T(8,128)S(1)} %collective-permute-done.5.after, f32[8,32,128]{2,1,0:T(8,128)S(1)} %collective-permute-done.6.z_after, ...), custom_call_target="tpu_custom_call" | custom-call | flops 1635778560 | bytes 4194304 | tf_op jit(solution)/shard_map/step1/pallas_call | solution.py:249
  112.0 26.5 %all_to_all.11.got = f32[16,128,128]{2,1,0:T(8,128)S(1)} all-to-all(f32[16,128,128]{2,1,0:T(8,128)S(1)} %step1.1), channel_id=1, replica_groups=mesh['space'=32,'field'=16] {'field'}, dimensions={0} | all-to-all | bytes 2097152 | tf_op jit(solution)/shard_map/all_to_all | solution.py:263
  138.4 5.0 %close.1 = f32[4,16,32,128]{3,2,1,0:T(8,128)S(1)} custom-call(f32[16,128,128]{2,1,0:T(8,128)S(1)} %all_to_all.11.got), custom_call_target="tpu_custom_call" | custom-call | tf_op jit(solution)/shard_map/close/pallas_call | solution.py:264
  143.4 1.6 %copy.32 = f32[1,32,4,16,128]{4,3,2,1,0:T(8,128)} copy(f32[1,32,4,16,128]{4,1,3,2,0:T(8,128)S(1)} %bitcast.10) | data formatting | bytes 2097152 | tf_op jit(solution)/shard_map/broadcast_in_dim | solution.py:265
  (18 shorter events, 0.1 us)
Async XLA Ops:
  0.0 1.9 %copy-start.4 = (f32[2,1,3]{2,1,0:T(1,128)S(1)}, f32[2,1,3]{2,1,0:T(1,128)}, u32[]{:S(2)}) copy-start(f32[2,1,3]{2,1,0:T(1,128)} %jumps.1) | copy-start | bytes 76
  0.0 1.9 %copy-start.3 = (f32[4,1,128]{2,1,0:T(1,128)S(1)}, f32[4,1,128]{2,1,0:T(1,128)}, u32[]{:S(2)}) copy-start(f32[4,1,128]{2,1,0:T(1,128)} %therm.1) | copy-start | bytes 6148
  0.0 1.9 %copy-start.2 = (f32[4,1,128]{2,1,0:T(1,128)S(1)}, f32[4,1,128]{2,1,0:T(1,128)}, u32[]{:S(2)}) copy-start(f32[4,1,128]{2,1,0:T(1,128)} %mix.1) | copy-start | bytes 6148
  0.0 1.9 %copy-start.1 = (f32[4,1,128]{2,1,0:T(1,128)S(1)}, f32[4,1,128]{2,1,0:T(1,128)}, u32[]{:S(2)}) copy-start(f32[4,1,128]{2,1,0:T(1,128)} %spread.1) | copy-start | bytes 6148
  0.0 1.9 %copy-start = (f32[3,4,1,128]{3,2,1,0:T(1,128)S(1)}, f32[3,4,1,128]{3,2,1,0:T(1,128)}, u32[]{:S(2)}) copy-start(f32[3,4,1,128]{3,2,1,0:T(1,128)} %motion.1) | copy-start | bytes 18436
  35.3 18.2 %copy-start.6 = (bf16[206,32]{0,1:T(8,128)(2,1)S(1)}, bf16[206,32]{0,1:T(8,128)(2,1)}, u32[]{:S(2)}) copy-start(bf16[206,32]{0,1:T(8,128)(2,1)} %param.17) | copy-start | bytes 39556
  35.3 18.3 %copy-start.7 = (bf16[206,32]{0,1:T(8,128)(2,1)S(1)}, bf16[206,32]{0,1:T(8,128)(2,1)}, u32[]{:S(2)}) copy-start(bf16[206,32]{0,1:T(8,128)(2,1)} %param.18) | copy-start | bytes 39556
  35.3 18.4 %copy-start.8 = (f32[206]{0:T(256)S(1)}, f32[206]{0:T(256)}, u32[]{:S(2)}) copy-start(f32[206]{0:T(256)} %param.21) | copy-start | bytes 2476
  35.3 18.5 %copy-start.9 = (f32[206]{0:T(256)S(1)}, f32[206]{0:T(256)}, u32[]{:S(2)}) copy-start(f32[206]{0:T(256)} %param.20) | copy-start | bytes 2476
  35.3 20.1 %copy-start.5 = (bf16[32,206]{1,0:T(8,128)(2,1)S(1)}, bf16[32,206]{1,0:T(8,128)(2,1)}, u32[]{:S(2)}) copy-start(bf16[32,206]{1,0:T(8,128)(2,1)} %gain.3) | copy-start | bytes 39556
  35.9 19.5 %collective-permute-start = (f32[16,32,128]{2,1,0:T(8,128)S(1)}, f32[16,32,128]{2,1,0:T(8,128)S(1)}, u32[]{:S(2)}, u32[]{:S(2)}) collective-permute-start(f32[16,32,128]{2,1,0:T(8,128)S(1)} %get-tuple-element.16), channel_id=1, source_target_pairs={{0,16},{16,32},{32,48},{48,64},{64,80},{80,96},{96,112},{112,128},... | collective-permute-start | bytes 786440 | tf_op jit(solution)/shard_map/ppermute | solution.py:222
  37.8 17.6 %collective-permute-start.1 = (f32[16,32,128]{2,1,0:T(8,128)S(1)}, f32[16,32,128]{2,1,0:T(8,128)S(1)}, u32[]{:S(2)}, u32[]{:S(2)}) collective-permute-start(f32[16,32,128]{2,1,0:T(8,128)S(1)} %get-tuple-element.17), channel_id=1, source_target_pairs={{16,0},{32,16},{48,32},{64,48},{80,64},{96,80},{112,96},{128,112},... | collective-permute-start | bytes 786440 | tf_op jit(solution)/shard_map/ppermute | solution.py:222
  47.9 6.3 %collective-permute-start.2 = (f32[8,32,128]{2,1,0:T(8,128)S(1)}, f32[8,32,128]{2,1,0:T(8,128)S(1)}, u32[]{:S(2)}, u32[]{:S(2)}) collective-permute-start(f32[8,32,128]{2,1,0:T(8,128)S(1)} %get-tuple-element.18), channel_id=1, source_target_pairs={{1,0},{2,1},{3,2},{4,3},{5,4},{6,5},{7,6},{8,7},{9,8},{10,9},{11,1... | collective-permute-start | bytes 393224 | tf_op jit(solution)/shard_map/ppermute | solution.py:222
  50.5 4.9 %collective-permute-start.3 = (f32[8,32,128]{2,1,0:T(8,128)S(1)}, f32[8,32,128]{2,1,0:T(8,128)S(1)}, u32[]{:S(2)}, u32[]{:S(2)}) collective-permute-start(f32[8,32,128]{2,1,0:T(8,128)S(1)} %get-tuple-element.19), channel_id=1, source_target_pairs={{0,1},{1,2},{2,3},{3,4},{4,5},{5,6},{6,7},{7,8},{8,9},{9,10},{10,1... | collective-permute-start | bytes 393224 | tf_op jit(solution)/shard_map/ppermute | solution.py:222
  73.5 20.8 %collective-permute-start.4 = (f32[16,32,128]{2,1,0:T(8,128)S(1)}, f32[16,32,128]{2,1,0:T(8,128)S(1)}, u32[]{:S(2)}, u32[]{:S(2)}) collective-permute-start(f32[16,32,128]{2,1,0:T(8,128)S(1)} %get-tuple-element.23), channel_id=1, source_target_pairs={{0,16},{16,32},{32,48},{48,64},{64,80},{80,96},{96,112},{112,128},... | collective-permute-start | bytes 786440 | tf_op jit(solution)/shard_map/ppermute | solution.py:222
  75.5 18.9 %collective-permute-start.5 = (f32[16,32,128]{2,1,0:T(8,128)S(1)}, f32[16,32,128]{2,1,0:T(8,128)S(1)}, u32[]{:S(2)}, u32[]{:S(2)}) collective-permute-start(f32[16,32,128]{2,1,0:T(8,128)S(1)} %get-tuple-element.24), channel_id=1, source_target_pairs={{16,0},{32,16},{48,32},{64,48},{80,64},{96,80},{112,96},{128,112},... | collective-permute-start | bytes 786440 | tf_op jit(solution)/shard_map/ppermute | solution.py:222
  81.6 10.1 %collective-permute-start.6 = (f32[8,32,128]{2,1,0:T(8,128)S(1)}, f32[8,32,128]{2,1,0:T(8,128)S(1)}, u32[]{:S(2)}, u32[]{:S(2)}) collective-permute-start(f32[8,32,128]{2,1,0:T(8,128)S(1)} %get-tuple-element.25), channel_id=1, source_target_pairs={{1,0},{2,1},{3,2},{4,3},{5,4},{6,5},{7,6},{8,7},{9,8},{10,9},{11,1... | collective-permute-start | bytes 393224 | tf_op jit(solution)/shard_map/ppermute | solution.py:222
  89.7 4.6 %collective-permute-start.7 = (f32[8,32,128]{2,1,0:T(8,128)S(1)}, f32[8,32,128]{2,1,0:T(8,128)S(1)}, u32[]{:S(2)}, u32[]{:S(2)}) collective-permute-start(f32[8,32,128]{2,1,0:T(8,128)S(1)} %get-tuple-element.26), channel_id=1, source_target_pairs={{0,1},{1,2},{2,3},{3,4},{4,5},{5,6},{6,7},{7,8},{8,9},{9,10},{10,1... | collective-permute-start | bytes 393224 | tf_op jit(solution)/shard_map/ppermute | solution.py:222
